TPU v7x, 256 devices: a whole 4x4x8 slice. The times are simulated.
256 devices in a mesh: px: 4 (over y_lo, core), py: 8 (over x, y_hi), dom: 8 (over z).
Axes of the slice: x: 4, y: 4 (y_hi: 2, y_lo: 2; y = y_hi * 2 + y_lo), z: 8, core: 2. Of those that a mesh axis runs over, the one named last changes fastest.
Arguments:
- velocity: float32 [16, 64, 256, 128], P('dom', 'px', 'py'), may hold values from 0.65 to 2.2
- buoyancy: float32 [64, 256, 128], P('px', 'py'), may hold values from 0.6 to 1.6
- forward_prev: float32 [16, 64, 256, 128], P('dom', 'px', 'py'), may hold values from -12 to 12
- forward_now: float32 [16, 64, 256, 128], P('dom', 'px', 'py'), may hold values from -12 to 12
- adjoint_prev: float32 [16, 64, 256, 128], P('dom', 'px', 'py'), may hold values from -12 to 12
- adjoint_now: float32 [16, 64, 256, 128], P('dom', 'px', 'py'), may hold values from -12 to 12
- sources: int32 [16], P('dom'), may hold values from 0 to 2097151
- wavelet: float32 [16, 3], P('dom'), may hold values from -800 to 800
- receivers: int32 [16, 1024], P('dom'), may hold values from 0 to 2097151
- misfit: float32 [16, 3, 1024], P('dom'), may hold values from -6 to 6
- sponge: int32 [6], replicated, may hold values from 2 to 8
Outputs:
- forward_before: float32 [16, 64, 256, 128], P('dom', 'px', 'py')
- forward_after: float32 [16, 64, 256, 128], P('dom', 'px', 'py')
- adjoint_before: float32 [16, 64, 256, 128], P('dom', 'px', 'py')
- adjoint_after: float32 [16, 64, 256, 128], P('dom', 'px', 'py')
- drift: float32 [16, 64, 256, 128], P('dom', 'px', 'py')
- spread: float32 [16, 64, 256, 128], P('dom', 'px', 'py')
All inputs are finite; a program needn't handle non-finite values.
Results may differ from a plain program's by a relative error of at most 0.0003.
Values sent between devices are 32-bit elements; how exact they have to be, the bound alone decides.
A program may use at most 64 MiB of HBM per device.

v0:
```python
import jax
import jax.numpy as jnp
from jax import lax
from jax.sharding import PartitionSpec as P

EPSILON = 1e-06
TIME_STEP = 0.18
SPONGE_RATE = 0.5
NEAR_WEIGHT = 9.0 / 8.0
FAR_WEIGHT = 1.0 / 24.0


def with_halo(cells, sides, width):
    for axis, dim in sides:
        count = lax.axis_size(axis)
        ends = count - 1
        head = lax.slice_in_dim(cells, 0, width, axis=dim)
        tail = lax.slice_in_dim(cells, cells.shape[dim] - width, cells.shape[dim], axis=dim)
        cells = jnp.concatenate(
            [
                lax.ppermute(tail, axis, [(i, (i + 1) % count) for i in range(ends)]),
                cells,
                lax.ppermute(head, axis, [((i + 1) % count, i) for i in range(ends)]),
            ],
            axis=dim,
        )
    return cells


def take_slab(source_array, start_at, amount, which_axis):
    return lax.slice_in_dim(
        source_array, start_at, start_at + amount, axis=source_array.ndim + which_axis
    )


def axis_term(wave_field, buoy_field, extent, which_axis):
    half_buoy = 0.5 * (
        take_slab(buoy_field, 1, extent + 3, which_axis)
        + take_slab(buoy_field, 2, extent + 3, which_axis)
    )
    slope_face = NEAR_WEIGHT * (
        take_slab(wave_field, 2, extent + 3, which_axis)
        - take_slab(wave_field, 1, extent + 3, which_axis)
    ) - FAR_WEIGHT * (
        take_slab(wave_field, 3, extent + 3, which_axis)
        - take_slab(wave_field, 0, extent + 3, which_axis)
    )
    flux_face = half_buoy * slope_face
    return NEAR_WEIGHT * (
        take_slab(flux_face, 2, extent, which_axis) - take_slab(flux_face, 1, extent, which_axis)
    ) - FAR_WEIGHT * (
        take_slab(flux_face, 3, extent, which_axis) - take_slab(flux_face, 0, extent, which_axis)
    )


def divergence(padded, buoy_pad):
    size_x = padded.shape[-3] - 6
    size_y = padded.shape[-2] - 6
    size_z = padded.shape[-1] - 6
    along_x = axis_term(
        padded[..., 3 : size_y + 3, 3 : size_z + 3],
        buoy_pad[:, 3 : size_y + 3, 3 : size_z + 3],
        size_x,
        -3,
    )
    along_y = axis_term(
        padded[..., 3 : size_x + 3, :, 3 : size_z + 3],
        buoy_pad[3 : size_x + 3, :, 3 : size_z + 3],
        size_y,
        -2,
    )
    along_z = axis_term(
        padded[..., 3 : size_x + 3, 3 : size_y + 3, :],
        buoy_pad[3 : size_x + 3, 3 : size_y + 3, :],
        size_z,
        -1,
    )
    return along_x + along_y + along_z


def sponge_term(coords, length, low_width, high_width):
    position = coords.astype(jnp.float32)
    far_side = length - 1 - position
    low_float = low_width.astype(jnp.float32)
    high_float = high_width.astype(jnp.float32)
    low_part = jnp.where(
        position < low_float, jnp.square(SPONGE_RATE * (low_float - position) / low_float), 0.0
    )
    high_part = jnp.where(
        far_side < high_float, jnp.square(SPONGE_RATE * (high_float - far_side) / high_float), 0.0
    )
    return low_part + high_part


def plane_tables(flat_index, size_x, size_y, size_z, total_y):
    plane_size = total_y * size_z
    global_x = flat_index // plane_size
    global_y = flat_index // size_z % total_y
    global_z = flat_index % size_z
    local_x = global_x - lax.axis_index("px") * size_x
    local_y = global_y - lax.axis_index("py") * size_y
    inside = (local_x >= 0) & (local_x < size_x) & (local_y >= 0) & (local_y < size_y)
    plane_at = jnp.where(inside, local_x * size_y + local_y, -1)
    plane_hot = (plane_at[..., None] == lax.iota(jnp.int32, size_x * size_y)).astype(jnp.float32)
    depth_hot = (global_z[..., None] == lax.iota(jnp.int32, size_z)).astype(jnp.float32)
    return (plane_hot, depth_hot)


def kernel_from(gram_total, particles):
    diag_part = jnp.diagonal(gram_total)
    dist_sq = diag_part[:, None] + diag_part[None, :] - 2.0 * gram_total
    width = jnp.sum(dist_sq) / (particles * (particles - 1)) + EPSILON
    kernel = jnp.exp(-dist_sq / width)
    return (kernel, jnp.sum(kernel, axis=1))


def on_device(
    velocity,
    buoyancy,
    forward_prev,
    forward_now,
    adjoint_prev,
    adjoint_now,
    sources,
    wavelet,
    receivers,
    misfit,
    sponge,
):
    part_dev, size_x, size_y, size_z = velocity.shape
    block_cells = size_x * size_y * size_z
    total_x = size_x * lax.axis_size("px")
    total_y = size_y * lax.axis_size("py")
    total_cells = total_x * total_y * size_z
    particles = part_dev * lax.axis_size("dom")
    step_sq = TIME_STEP * TIME_STEP
    coords_x = lax.iota(jnp.int32, size_x) + lax.axis_index("px") * size_x
    coords_y = lax.iota(jnp.int32, size_y) + lax.axis_index("py") * size_y
    coords_z = lax.iota(jnp.int32, size_z)
    damping = jnp.exp(
        -(
            sponge_term(coords_x, total_x, sponge[0], sponge[1])[:, None, None]
            + sponge_term(coords_y, total_y, sponge[2], sponge[3])[None, :, None]
            + sponge_term(coords_z, size_z, sponge[4], sponge[5])[None, None, :]
        )
    )
    buoy_rim = with_halo(buoyancy, (("px", 0), ("py", 1)), 3)
    buoy_pad = jnp.pad(buoy_rim, ((0, 0), (0, 0), (3, 3)))
    wave_scale = velocity * velocity / buoyancy
    grad_coef = -2.0 / (velocity * velocity * velocity)
    src_plane, src_depth = plane_tables(sources, size_x, size_y, size_z, total_y)
    src_pattern = (src_plane[:, :, None] * src_depth[:, None, :]).reshape(velocity.shape)
    rec_plane, rec_depth = plane_tables(receivers, size_x, size_y, size_z, total_y)
    previous = jnp.stack([forward_prev, adjoint_prev])
    current = jnp.stack([forward_now, adjoint_now])
    gradient = jnp.zeros_like(velocity)
    for step_at in range(wavelet.shape[1]):
        rimmed = with_halo(current, (("px", 2), ("py", 3)), 3)
        padded = jnp.pad(rimmed, ((0, 0), (0, 0), (0, 0), (0, 0), (3, 3)))
        stepped = 2.0 * current - previous + step_sq * (wave_scale * divergence(padded, buoy_pad))
        weighted_depth = rec_depth * (step_sq * misfit[:, step_at, :])[:, :, None]
        rec_field = jnp.einsum(
            "prq,prz->pqz",
            rec_plane,
            weighted_depth,
            precision=lax.Precision.HIGHEST,
            preferred_element_type=jnp.float32,
        )
        src_field = src_pattern * (step_sq * wavelet[:, step_at])[:, None, None, None]
        injected = jnp.stack(
            [stepped[0] + src_field, stepped[1] + rec_field.reshape(velocity.shape)]
        )
        advanced = damping * injected
        gradient = gradient + grad_coef * current[1] * (
            advanced[0] - 2.0 * current[0] + previous[0]
        )
        previous, current = (current, advanced)
    flat_model = velocity.reshape(part_dev, block_cells)
    flat_grad = gradient.reshape(part_dev, block_cells)
    dom_start = lax.axis_index("dom") * part_dev
    own_sq = lax.psum(jnp.sum(flat_grad * flat_grad, axis=1), ("px", "py"))
    flat_grad = flat_grad / jnp.sqrt(own_sq / total_cells + EPSILON)[:, None]
    model_cols, grad_cols = (
        lax.all_to_all(flat_model, "dom", split_axis=1, concat_axis=0, tiled=True),
        lax.all_to_all(flat_grad, "dom", split_axis=1, concat_axis=0, tiled=True),
    )
    centered = model_cols - jnp.mean(model_cols, axis=0, keepdims=True)
    gram_part = jnp.dot(
        centered, centered.T, precision=lax.Precision.HIGHEST, preferred_element_type=jnp.float32
    )
    gram_total = lax.psum(gram_part, ("px", "py", "dom"))
    kernel, row_sum = kernel_from(gram_total, particles)
    mixed_grad = jnp.dot(
        kernel, grad_cols, precision=lax.Precision.HIGHEST, preferred_element_type=jnp.float32
    )
    mixed_model = jnp.dot(
        kernel, model_cols, precision=lax.Precision.HIGHEST, preferred_element_type=jnp.float32
    )
    drift_flat, model_mix = (
        lax.all_to_all(mixed_grad, "dom", split_axis=0, concat_axis=1, tiled=True),
        lax.all_to_all(mixed_model, "dom", split_axis=0, concat_axis=1, tiled=True),
    )
    own_rowsum = lax.dynamic_slice_in_dim(row_sum, dom_start, part_dev)
    spread_flat = flat_model * own_rowsum[:, None] - model_mix
    return (
        previous[0],
        current[0],
        previous[1],
        current[1],
        drift_flat.reshape(velocity.shape),
        spread_flat.reshape(velocity.shape),
    )


def solution(mesh):
    placed = (
        P("dom", "px", "py", None),
        P("px", "py", None),
        P("dom", "px", "py", None),
        P("dom", "px", "py", None),
        P("dom", "px", "py", None),
        P("dom", "px", "py", None),
        P("dom"),
        P("dom", None),
        P("dom", None),
        P("dom", None, None),
        P(),
    )
    return jax.shard_map(
        on_device,
        mesh=mesh,
        in_specs=placed,
        out_specs=(
            P("dom", "px", "py", None),
            P("dom", "px", "py", None),
            P("dom", "px", "py", None),
            P("dom", "px", "py", None),
            P("dom", "px", "py", None),
            P("dom", "px", "py", None),
        ),
        check_vma=False,
    )
```

profile of v0, /device:TPU:1, one launch (start us, length us, event | category | flops | bytes accessed | tf_op | source)
XLA Modules:
  0.0 337.7 jit_solution(8753166672885361764)
XLA Ops:
  2.5 5.1 %collective-permute-start.3 = (f32[2,2,3,32,128]{4,3,2,1,0:T(8,128)}, f32[2,2,3,32,128]{4,3,2,1,0:T(8,128)S(1)}, u32[]{:S(2)}, u32[]{:S(2)}) collective-permute-start(f32[2,2,3,32,128]{4,3,2,1,0:T(8,128)} %get-tuple-element.33), channel_id=1, source_target_pairs={{64,0},{128,64},{192,128},{65,1},{129,65},{193,129},{66,2},{130,66... | collective-permute-start | bytes 589832 | tf_op jit(solution)/shard_map/ppermute | solution.py:23
  15.3 7.7 %all-to-all-start = ((f32[2,8,8192]{2,0,1:T(2,128)}), f32[2,8,8192]{2,0,1:T(2,128)S(1)}, u32[]{:S(2)}, u32[]{:S(2)}) async-start(f32[2,8,8192]{2,0,1:T(2,128)} %copy.54), calls=%async_computation | async-start | bytes 1048576 | tf_op jit(solution)/shard_map/all_to_all | solution.py:184
  28.1 3.2 fusion.2
  32.7 5.5 %collective-permute-start.4 = (f32[22,3,128]{2,1,0:T(4,128)S(1)}, f32[22,3,128]{2,1,0:T(4,128)S(1)}, u32[]{:S(2)}, u32[]{:S(2)}) collective-permute-start(f32[22,3,128]{2,1,0:T(4,128)S(1)} %get-tuple-element.36), channel_id=1, source_target_pairs={{0,8},{8,16},{16,24},{24,32},{32,40},{40,48},{48,56},{1,9},{9,17},... | collective-permute-start | bytes 101384 | tf_op jit(solution)/shard_map/ppermute | solution.py:21
  42.3 6.9 %collective-permute-start.6 = (f32[2,2,22,3,128]{4,3,2,1,0:T(4,128)}, f32[2,2,22,3,128]{4,3,2,1,0:T(4,128)}, u32[]{:S(2)}, u32[]{:S(2)}) collective-permute-start(f32[2,2,22,3,128]{4,3,2,1,0:T(4,128)} %get-tuple-element.20), channel_id=1, source_target_pairs={{0,8},{8,16},{16,24},{24,32},{32,40},{40,48},{48,56},{1,9},{9,17},... | collective-permute-start | bytes 405512 | tf_op jit(solution)/shard_map/ppermute | solution.py:21
  54.3 79.6 %psum.14 = f32[16,16]{1,0:T(8,128)S(1)} all-reduce(f32[16,16]{1,0:T(8,128)S(1)} %fusion.141), channel_id=1, replica_groups=mesh['px'=4,'py'=8,'dom'=8] {'px','py','dom'}, use_global_device_ids=true, to_apply=%region_1.2 | all-reduce | flops 256 | bytes 2048 | tf_op jit(solution)/shard_map/psum | solution.py:191
  137.9 5.5 %all-to-all-start.3 = ((f32[8,2,8192]{2,1,0:T(2,128)}), f32[8,2,8192]{2,1,0:T(2,128)}, u32[]{:S(2)}, u32[]{:S(2)}) async-start(f32[8,2,8192]{2,1,0:T(2,128)} %copy.60), calls=%async_computation.3 | async-start | bytes 1048576 | tf_op jit(solution)/shard_map/all_to_all | solution.py:201
  143.3 2.4 fusion.47
  147.1 3.1 fusion.6
  150.2 2.6 fusion.37
  152.8 8.6 %all-to-all-done.3 = f32[8,2,8192]{2,1,0:T(2,128)} async-done(((f32[8,2,8192]{2,1,0:T(2,128)}), f32[8,2,8192]{2,1,0:T(2,128)}, u32[]{:S(2)}, u32[]{:S(2)}) %all-to-all-start.3) | async-done | bytes 524320 | tf_op jit(solution)/shard_map/all_to_all | solution.py:201
  167.8 4.3 %fusion.84 = f32[2,2,16,32,128]{4,3,2,1,0:T(8,128)S(1)} fusion(f32[2,2,16,32,131]{4,3,2,1,0:T(8,128)} %fusion.6, f32[2,2,16,35,128]{4,3,2,1,0:T(8,128)S(1)} %copy-done.2, f32[2,2,19,32,128]{4,3,2,1,0:T(8,128)S(1)} %fusion.47, f32[1,2,16,32,128]{4,3,2,1,0:T(8,128)S(1)} %bitcast.82, f32[1,2,16,32,128]{4,3,2,1,0:T(8,128)S(1)} %bitcast.81, ...), kind=kLoop, calls=%fused_computation.153 | loop fusion | flops 6291456 | bytes 16252928 | tf_op jit(solution)/shard_map/add | solution.py:160
  175.0 3.2 collective-permute-start.8
  178.2 2.5 fusion.1
  182.1 5.6 %collective-permute-start.10 = (f32[2,2,22,3,128]{4,3,2,1,0:T(4,128)S(1)}, f32[2,2,22,3,128]{4,3,2,1,0:T(4,128)S(1)}, u32[]{:S(2)}, u32[]{:S(2)}) collective-permute-start(f32[2,2,22,3,128]{4,3,2,1,0:T(4,128)S(1)} %get-tuple-element.18), channel_id=1, source_target_pairs={{0,8},{8,16},{16,24},{24,32},{32,40},{40,48},{48,56},{1,9},{9,17},... | collective-permute-start | bytes 405512 | tf_op jit(solution)/shard_map/ppermute | solution.py:21
  190.2 2.4 collective-permute-done.10
  199.2 3.5 %collective-permute-start.12 = (f32[2,2,3,32,128]{4,3,2,1,0:T(8,128)S(1)}, f32[2,2,3,32,128]{4,3,2,1,0:T(8,128)S(1)}, u32[]{:S(2)}, u32[]{:S(2)}) collective-permute-start(f32[2,2,3,32,128]{4,3,2,1,0:T(8,128)S(1)} %get-tuple-element.24), channel_id=1, source_target_pairs={{0,64},{64,128},{128,192},{1,65},{65,129},{129,193},{2,66},{66,130... | collective-permute-start | bytes 589832 | tf_op jit(solution)/shard_map/ppermute | solution.py:21
  202.7 2.5 fusion
  206.6 6.3 %collective-permute-start.14 = (f32[2,2,22,3,128]{4,3,2,1,0:T(4,128)S(1)}, f32[2,2,22,3,128]{4,3,2,1,0:T(4,128)S(1)}, u32[]{:S(2)}, u32[]{:S(2)}) collective-permute-start(f32[2,2,22,3,128]{4,3,2,1,0:T(4,128)S(1)} %get-tuple-element.16), channel_id=1, source_target_pairs={{0,8},{8,16},{16,24},{24,32},{32,40},{40,48},{48,56},{1,9},{9,17},... | collective-permute-start | bytes 405512 | tf_op jit(solution)/shard_map/ppermute | solution.py:21
  215.1 4.6 %collective-permute-done.14 = f32[2,2,22,3,128]{4,3,2,1,0:T(4,128)S(1)} collective-permute-done((f32[2,2,22,3,128]{4,3,2,1,0:T(4,128)S(1)}, f32[2,2,22,3,128]{4,3,2,1,0:T(4,128)S(1)}, u32[]{:S(2)}, u32[]{:S(2)}) %collective-permute-start.14) | collective-permute-done | bytes 135200 | tf_op jit(solution)/shard_map/ppermute | solution.py:21
  226.5 68.9 %psum.15 = f32[2]{0:T(128)S(1)} all-reduce(f32[2]{0:T(128)S(1)} %get-tuple-element.11), channel_id=1, replica_groups=mesh['px'=4,'py'=8,'dom'=8] {'px','py'}, use_global_device_ids=true, to_apply=%region_4.5 | all-reduce | flops 2 | bytes 16 | tf_op jit(solution)/shard_map/psum | solution.py:181
  295.9 19.1 %all_to_all.64 = f32[2,8,8192]{2,0,1:T(2,128)S(1)} all-to-all(f32[2,8,8192]{2,0,1:T(2,128)S(1)} %copy.55), channel_id=1, replica_groups=mesh['px'=4,'py'=8,'dom'=8] {'dom'}, dimensions={1} | all-to-all | bytes 1048576 | tf_op jit(solution)/shard_map/all_to_all | solution.py:185
  317.1 3.5 %all-to-all-start.2 = ((f32[8,2,8192]{2,1,0:T(2,128)}), f32[8,2,8192]{2,1,0:T(2,128)S(1)}, u32[]{:S(2)}, u32[]{:S(2)}) async-start(f32[8,2,8192]{2,1,0:T(2,128)} %copy.57), calls=%async_computation.2 | async-start | bytes 1048576 | tf_op jit(solution)/shard_map/all_to_all | solution.py:200
  321.5 15.1 %all-to-all-done.2 = f32[8,2,8192]{2,1,0:T(2,128)S(1)} async-done(((f32[8,2,8192]{2,1,0:T(2,128)}), f32[8,2,8192]{2,1,0:T(2,128)S(1)}, u32[]{:S(2)}, u32[]{:S(2)}) %all-to-all-start.2) | async-done | bytes 524320 | tf_op jit(solution)/shard_map/all_to_all | solution.py:200
  (139 shorter events, 60.4 us)
Async XLA Ops:
  0.6 13.2 %copy-start.8 = (f32[2,16,32,128]{3,2,1,0:T(8,128)S(1)}, f32[2,16,32,128]{3,2,1,0:T(8,128)}, u32[]{:S(2)}) copy-start(f32[2,16,32,128]{3,2,1,0:T(8,128)} %param.11) | copy-start | bytes 1572868
  2.5 37.4 %collective-permute-start.3 = (f32[2,2,3,32,128]{4,3,2,1,0:T(8,128)}, f32[2,2,3,32,128]{4,3,2,1,0:T(8,128)S(1)}, u32[]{:S(2)}, u32[]{:S(2)}) collective-permute-start(f32[2,2,3,32,128]{4,3,2,1,0:T(8,128)} %get-tuple-element.33), channel_id=1, source_target_pairs={{64,0},{128,64},{192,128},{65,1},{129,65},{193,129},{66,2},{130,66... | collective-permute-start | bytes 589832 | tf_op jit(solution)/shard_map/ppermute | solution.py:23
  7.6 32.3 %collective-permute-start.2 = (f32[2,2,3,32,128]{4,3,2,1,0:T(8,128)S(1)}, f32[2,2,3,32,128]{4,3,2,1,0:T(8,128)S(1)}, u32[]{:S(2)}, u32[]{:S(2)}) collective-permute-start(f32[2,2,3,32,128]{4,3,2,1,0:T(8,128)S(1)} %get-tuple-element.32), channel_id=1, source_target_pairs={{0,64},{64,128},{128,192},{1,65},{65,129},{129,193},{2,66},{66,130... | collective-permute-start | bytes 589832 | tf_op jit(solution)/shard_map/ppermute | solution.py:21
  9.5 21.8 %collective-permute-start = (f32[3,32,128]{2,1,0:T(8,128)S(1)}, f32[3,32,128]{2,1,0:T(8,128)S(1)}, u32[]{:S(2)}, u32[]{:S(2)}) collective-permute-start(f32[3,32,128]{2,1,0:T(8,128)S(1)} %get-tuple-element.39), channel_id=1, source_target_pairs={{0,64},{64,128},{128,192},{1,65},{65,129},{129,193},{2,66},{66,130... | collective-permute-start | bytes 147464 | tf_op jit(solution)/shard_map/ppermute | solution.py:21
  11.5 19.9 %collective-permute-start.1 = (f32[3,32,128]{2,1,0:T(8,128)S(1)}, f32[3,32,128]{2,1,0:T(8,128)S(1)}, u32[]{:S(2)}, u32[]{:S(2)}) collective-permute-start(f32[3,32,128]{2,1,0:T(8,128)S(1)} %get-tuple-element.38), channel_id=1, source_target_pairs={{64,0},{128,64},{192,128},{65,1},{129,65},{193,129},{66,2},{130,66... | collective-permute-start | bytes 147464 | tf_op jit(solution)/shard_map/ppermute | solution.py:23
  14.0 9.3 %copy-start.14 = (f32[2,3,1024]{2,0,1:T(2,128)S(1)}, f32[2,3,1024]{2,0,1:T(2,128)}, u32[]{:S(2)}) copy-start(f32[2,3,1024]{2,0,1:T(2,128)} %param.20) | copy-start | bytes 73732
  14.0 9.3 %copy-start.15 = (s32[6]{0:T(128)S(1)}, s32[6]{0:T(128)}, u32[]{:S(2)}) copy-start(s32[6]{0:T(128)} %param.21) | copy-start | bytes 76
  15.3 35.2 %all-to-all-start = ((f32[2,8,8192]{2,0,1:T(2,128)}), f32[2,8,8192]{2,0,1:T(2,128)S(1)}, u32[]{:S(2)}, u32[]{:S(2)}) async-start(f32[2,8,8192]{2,0,1:T(2,128)} %copy.54), calls=%async_computation | async-start | bytes 1048576 | tf_op jit(solution)/shard_map/all_to_all | solution.py:184
  31.4 7.6 %collective-permute-start.5 = (f32[22,3,128]{2,1,0:T(4,128)S(1)}, f32[22,3,128]{2,1,0:T(4,128)S(1)}, u32[]{:S(2)}, u32[]{:S(2)}) collective-permute-start(f32[22,3,128]{2,1,0:T(4,128)S(1)} %get-tuple-element.37), channel_id=1, source_target_pairs={{8,0},{16,8},{24,16},{32,24},{40,32},{48,40},{56,48},{9,1},{17,9},... | collective-permute-start | bytes 101384 | tf_op jit(solution)/shard_map/ppermute | solution.py:23
  32.7 6.6 %collective-permute-start.4 = (f32[22,3,128]{2,1,0:T(4,128)S(1)}, f32[22,3,128]{2,1,0:T(4,128)S(1)}, u32[]{:S(2)}, u32[]{:S(2)}) collective-permute-start(f32[22,3,128]{2,1,0:T(4,128)S(1)} %get-tuple-element.36), channel_id=1, source_target_pairs={{0,8},{8,16},{16,24},{24,32},{32,40},{40,48},{48,56},{1,9},{9,17},... | collective-permute-start | bytes 101384 | tf_op jit(solution)/shard_map/ppermute | solution.py:21
  39.9 10.6 %copy-start.4 = (f32[2,2,3,32,128]{4,3,2,1,0:T(8,128)}, f32[2,2,3,32,128]{4,3,2,1,0:T(8,128)S(1)}, u32[]{:S(2)}) copy-start(f32[2,2,3,32,128]{4,3,2,1,0:T(8,128)S(1)} %collective-permute-done.3) | copy-start | bytes 589828
  40.2 10.3 %copy-start.6 = (f32[2,2,3,32,128]{4,3,2,1,0:T(8,128)}, f32[2,2,3,32,128]{4,3,2,1,0:T(8,128)S(1)}, u32[]{:S(2)}) copy-start(f32[2,2,3,32,128]{4,3,2,1,0:T(8,128)S(1)} %collective-permute-done.2) | copy-start | bytes 589828
  41.0 104.7 %collective-permute-start.7 = (f32[2,2,22,3,128]{4,3,2,1,0:T(4,128)}, f32[2,2,22,3,128]{4,3,2,1,0:T(4,128)}, u32[]{:S(2)}, u32[]{:S(2)}) collective-permute-start(f32[2,2,22,3,128]{4,3,2,1,0:T(4,128)} %get-tuple-element.21), channel_id=1, source_target_pairs={{8,0},{16,8},{24,16},{32,24},{40,32},{48,40},{56,48},{9,1},{17,9},... | collective-permute-start | bytes 405512 | tf_op jit(solution)/shard_map/ppermute | solution.py:23
  42.3 103.5 %collective-permute-start.6 = (f32[2,2,22,3,128]{4,3,2,1,0:T(4,128)}, f32[2,2,22,3,128]{4,3,2,1,0:T(4,128)}, u32[]{:S(2)}, u32[]{:S(2)}) collective-permute-start(f32[2,2,22,3,128]{4,3,2,1,0:T(4,128)} %get-tuple-element.20), channel_id=1, source_target_pairs={{0,8},{8,16},{16,24},{24,32},{32,40},{40,48},{48,56},{1,9},{9,17},... | collective-permute-start | bytes 405512 | tf_op jit(solution)/shard_map/ppermute | solution.py:21
  137.9 23.5 %all-to-all-start.3 = ((f32[8,2,8192]{2,1,0:T(2,128)}), f32[8,2,8192]{2,1,0:T(2,128)}, u32[]{:S(2)}, u32[]{:S(2)}) async-start(f32[8,2,8192]{2,1,0:T(2,128)} %copy.60), calls=%async_computation.3 | async-start | bytes 1048576 | tf_op jit(solution)/shard_map/all_to_all | solution.py:201
  172.6 8.1 %collective-permute-start.9 = (f32[2,2,3,32,128]{4,3,2,1,0:T(8,128)S(1)}, f32[2,2,3,32,128]{4,3,2,1,0:T(8,128)S(1)}, u32[]{:S(2)}, u32[]{:S(2)}) collective-permute-start(f32[2,2,3,32,128]{4,3,2,1,0:T(8,128)S(1)} %get-tuple-element.29), channel_id=1, source_target_pairs={{64,0},{128,64},{192,128},{65,1},{129,65},{193,129},{66,2},{130,66... | collective-permute-start | bytes 589832 | tf_op jit(solution)/shard_map/ppermute | solution.py:23
  175.0 5.8 %collective-permute-start.8 = (f32[2,2,3,32,128]{4,3,2,1,0:T(8,128)S(1)}, f32[2,2,3,32,128]{4,3,2,1,0:T(8,128)S(1)}, u32[]{:S(2)}, u32[]{:S(2)}) collective-permute-start(f32[2,2,3,32,128]{4,3,2,1,0:T(8,128)S(1)} %get-tuple-element.28), channel_id=1, source_target_pairs={{0,64},{64,128},{128,192},{1,65},{65,129},{129,193},{2,66},{66,130... | collective-permute-start | bytes 589832 | tf_op jit(solution)/shard_map/ppermute | solution.py:21
  180.8 9.3 %collective-permute-start.11 = (f32[2,2,22,3,128]{4,3,2,1,0:T(4,128)S(1)}, f32[2,2,22,3,128]{4,3,2,1,0:T(4,128)S(1)}, u32[]{:S(2)}, u32[]{:S(2)}) collective-permute-start(f32[2,2,22,3,128]{4,3,2,1,0:T(4,128)S(1)} %get-tuple-element.19), channel_id=1, source_target_pairs={{8,0},{16,8},{24,16},{32,24},{40,32},{48,40},{56,48},{9,1},{17,9},... | collective-permute-start | bytes 405512 | tf_op jit(solution)/shard_map/ppermute | solution.py:23
  182.1 10.5 %collective-permute-start.10 = (f32[2,2,22,3,128]{4,3,2,1,0:T(4,128)S(1)}, f32[2,2,22,3,128]{4,3,2,1,0:T(4,128)S(1)}, u32[]{:S(2)}, u32[]{:S(2)}) collective-permute-start(f32[2,2,22,3,128]{4,3,2,1,0:T(4,128)S(1)} %get-tuple-element.18), channel_id=1, source_target_pairs={{0,8},{8,16},{16,24},{24,32},{32,40},{40,48},{48,56},{1,9},{9,17},... | collective-permute-start | bytes 405512 | tf_op jit(solution)/shard_map/ppermute | solution.py:21
  196.9 8.3 %collective-permute-start.13 = (f32[2,2,3,32,128]{4,3,2,1,0:T(8,128)S(1)}, f32[2,2,3,32,128]{4,3,2,1,0:T(8,128)S(1)}, u32[]{:S(2)}, u32[]{:S(2)}) collective-permute-start(f32[2,2,3,32,128]{4,3,2,1,0:T(8,128)S(1)} %get-tuple-element.25), channel_id=1, source_target_pairs={{64,0},{128,64},{192,128},{65,1},{129,65},{193,129},{66,2},{130,66... | collective-permute-start | bytes 589832 | tf_op jit(solution)/shard_map/ppermute | solution.py:23
  199.2 6.0 %collective-permute-start.12 = (f32[2,2,3,32,128]{4,3,2,1,0:T(8,128)S(1)}, f32[2,2,3,32,128]{4,3,2,1,0:T(8,128)S(1)}, u32[]{:S(2)}, u32[]{:S(2)}) collective-permute-start(f32[2,2,3,32,128]{4,3,2,1,0:T(8,128)S(1)} %get-tuple-element.24), channel_id=1, source_target_pairs={{0,64},{64,128},{128,192},{1,65},{65,129},{129,193},{2,66},{66,130... | collective-permute-start | bytes 589832 | tf_op jit(solution)/shard_map/ppermute | solution.py:21
  205.3 9.8 %collective-permute-start.15 = (f32[2,2,22,3,128]{4,3,2,1,0:T(4,128)S(1)}, f32[2,2,22,3,128]{4,3,2,1,0:T(4,128)S(1)}, u32[]{:S(2)}, u32[]{:S(2)}) collective-permute-start(f32[2,2,22,3,128]{4,3,2,1,0:T(4,128)S(1)} %get-tuple-element.17), channel_id=1, source_target_pairs={{8,0},{16,8},{24,16},{32,24},{40,32},{48,40},{56,48},{9,1},{17,9},... | collective-permute-start | bytes 405512 | tf_op jit(solution)/shard_map/ppermute | solution.py:23
  206.6 13.1 %collective-permute-start.14 = (f32[2,2,22,3,128]{4,3,2,1,0:T(4,128)S(1)}, f32[2,2,22,3,128]{4,3,2,1,0:T(4,128)S(1)}, u32[]{:S(2)}, u32[]{:S(2)}) collective-permute-start(f32[2,2,22,3,128]{4,3,2,1,0:T(4,128)S(1)} %get-tuple-element.16), channel_id=1, source_target_pairs={{0,8},{8,16},{16,24},{24,32},{32,40},{40,48},{48,56},{1,9},{9,17},... | collective-permute-start | bytes 405512 | tf_op jit(solution)/shard_map/ppermute | solution.py:21
  317.1 19.4 %all-to-all-start.2 = ((f32[8,2,8192]{2,1,0:T(2,128)}), f32[8,2,8192]{2,1,0:T(2,128)S(1)}, u32[]{:S(2)}, u32[]{:S(2)}) async-start(f32[8,2,8192]{2,1,0:T(2,128)} %copy.57), calls=%async_computation.2 | async-start | bytes 1048576 | tf_op jit(solution)/shard_map/all_to_all | solution.py:200
  (14 other events, 61.7 us)
where the time goes:
time: 339 us; the launch traced here: 338 us
  blocking collectives  168 us (50%)
  starting transfers between devices  68.8 us (20%)
  other arithmetic  35.5 us (10%)
  waiting for transfers between devices  34.7 us (10%)
  local copies, waits for them, and re-layouts  15.2 us (4%)
  matrix products  10.2 us (3%)
  between operations  5.78 us (2%)
    psum x1, blocking collectives, on_device(): gram_total = lax.psum(gram_part, ('px', 'py', 'dom'))  79.6 us
    psum x1, blocking collectives, on_device(): own_sq = lax.psum(jnp.sum(flat_grad * flat_grad, axis=1), ('px', 'py'))  68.9 us
    ppermute x8, starting transfers between devices, with_halo(): lax.ppermute(tail, axis, [(i, (i + 1) % count) for i in range(ends)])  34.8 us
    all_to_all x1, blocking collectives, on_device(): lax.all_to_all(flat_grad, 'dom', split_axis=1, concat_axis=0, tiled=True)  19.1 us
    ppermute x8, starting transfers between devices, with_halo(): lax.ppermute(head, axis, [((i + 1) % count, i) for i in range(ends)])  17.4 us
    all_to_all x1, waiting for transfers between devices, on_device(): lax.all_to_all(mixed_grad, 'dom', split_axis=0, concat_axis=1, tiled=True)  15.1 us
    mul x9, other arithmetic, axis_term(): flux_face = half_buoy * slope_face  13.4 us
    all_to_all x1, waiting for transfers between devices, on_device(): lax.all_to_all(mixed_model, 'dom', split_axis=0, concat_axis=1, tiled=True)  8.58 us
  transfers between devices with their start and end apart: 19, of which 8 were waited for; matrix products, arithmetic and copies ran while one was open for 10% of the time, Pallas kernels for 0%

commit v1 on v0

--- a/solution.py
+++ b/solution.py
@@ -178,7 +178,7 @@
     flat_model = velocity.reshape(part_dev, block_cells)
     flat_grad = gradient.reshape(part_dev, block_cells)
     dom_start = lax.axis_index("dom") * part_dev
-    own_sq = lax.psum(jnp.sum(flat_grad * flat_grad, axis=1), ("px", "py"))
+    own_sq = lax.psum(lax.psum(jnp.sum(flat_grad * flat_grad, axis=1), "py"), "px")
     flat_grad = flat_grad / jnp.sqrt(own_sq / total_cells + EPSILON)[:, None]
     model_cols, grad_cols = (
         lax.all_to_all(flat_model, "dom", split_axis=1, concat_axis=0, tiled=True),

time: 339 us -> 299 us (0.88)
  blocking collectives: 168 us -> 127 us
    psum x1 -> x2, blocking collectives: 68.9 us -> 28.3 us  [the longest x1 19.1 us: on_device(): lax.psum(jnp.sum(flat_grad * flat_grad, axis=1), 'py')]
  transfers between devices with their start and end apart: 19 -> 19, of which waited for: 8 -> 8; matrix products, arithmetic and copies ran while one was open for 10% -> 11% of each run, Pallas kernels for 0% -> 0%
where the time goes in v1:
time: 299 us; the launch traced here: 297 us
  blocking collectives  127 us (42%)
  starting transfers between devices  68.8 us (23%)
  other arithmetic  35.5 us (12%)
  waiting for transfers between devices  34.7 us (12%)
  local copies, waits for them, and re-layouts  15.2 us (5%)
  matrix products  10.2 us (3%)
  between operations  5.87 us (2%)
    psum x1, blocking collectives, on_device(): gram_total = lax.psum(gram_part, ('px', 'py', 'dom'))  79.6 us
    ppermute x8, starting transfers between devices, with_halo(): lax.ppermute(tail, axis, [(i, (i + 1) % count) for i in range(ends)])  34.8 us
    all_to_all x1, blocking collectives, on_device(): lax.all_to_all(flat_grad, 'dom', split_axis=1, concat_axis=0, tiled=True)  19.2 us
    psum x1, blocking collectives, on_device(): lax.psum(jnp.sum(flat_grad * flat_grad, axis=1), 'py')  19.1 us
    ppermute x8, starting transfers between devices, with_halo(): lax.ppermute(head, axis, [((i + 1) % count, i) for i in range(ends)])  17.4 us
    all_to_all x1, waiting for transfers between devices, on_device(): lax.all_to_all(mixed_grad, 'dom', split_axis=0, concat_axis=1, tiled=True)  15.1 us
    mul x9, other arithmetic, axis_term(): flux_face = half_buoy * slope_face  13.4 us
    psum x1, blocking collectives, on_device(): lax.psum(lax.psum(jnp.sum(flat_grad * flat_grad, axis=1), 'py'), 'px')  9.17 us
  transfers between devices with their start and end apart: 19, of which 8 were waited for; matrix products, arithmetic and copies ran while one was open for 11% of the time, Pallas kernels for 0%

profile of v1, /device:TPU:1, one launch (start us, length us, event | category | flops | bytes accessed | tf_op | source)
XLA Modules:
  0.0 297.4 jit_solution(2518572764122210080)
XLA Ops:
  2.5 5.1 %collective-permute-start.3 = (f32[2,2,3,32,128]{4,3,2,1,0:T(8,128)}, f32[2,2,3,32,128]{4,3,2,1,0:T(8,128)S(1)}, u32[]{:S(2)}, u32[]{:S(2)}) collective-permute-start(f32[2,2,3,32,128]{4,3,2,1,0:T(8,128)} %get-tuple-element.33), channel_id=1, source_target_pairs={{64,0},{128,64},{192,128},{65,1},{129,65},{193,129},{66,2},{130,66... | collective-permute-start | bytes 589832 | tf_op jit(solution)/shard_map/ppermute | solution.py:23
  15.3 7.7 %all-to-all-start = ((f32[2,8,8192]{2,0,1:T(2,128)}), f32[2,8,8192]{2,0,1:T(2,128)S(1)}, u32[]{:S(2)}, u32[]{:S(2)}) async-start(f32[2,8,8192]{2,0,1:T(2,128)} %copy.54), calls=%async_computation | async-start | bytes 1048576 | tf_op jit(solution)/shard_map/all_to_all | solution.py:184
  28.3 3.2 %fusion.2 = f32[2,512,128]{2,1,0:T(8,128)} fusion(s32[2,1024]{1,0:T(2,128)S(1)} %get-tuple-element.44, f32[2,1024]{1,0:T(2,128)S(1)} %get-tuple-element.41, s32[2,1024]{1,0:T(2,128)S(1)} %get-tuple-element.43), kind=kOutput, calls=%fused_computation.16 | convolution fusion | flops 1612185600 | bytes 548864 | tf_op jit(solution)/shard_map/prq,prz->pqz/dot_general | solution.py:162
  32.9 5.5 %collective-permute-start.4 = (f32[22,3,128]{2,1,0:T(4,128)S(1)}, f32[22,3,128]{2,1,0:T(4,128)S(1)}, u32[]{:S(2)}, u32[]{:S(2)}) collective-permute-start(f32[22,3,128]{2,1,0:T(4,128)S(1)} %get-tuple-element.36), channel_id=1, source_target_pairs={{0,8},{8,16},{16,24},{24,32},{32,40},{40,48},{48,56},{1,9},{9,17},... | collective-permute-start | bytes 101384 | tf_op jit(solution)/shard_map/ppermute | solution.py:21
  42.5 6.9 %collective-permute-start.6 = (f32[2,2,22,3,128]{4,3,2,1,0:T(4,128)}, f32[2,2,22,3,128]{4,3,2,1,0:T(4,128)}, u32[]{:S(2)}, u32[]{:S(2)}) collective-permute-start(f32[2,2,22,3,128]{4,3,2,1,0:T(4,128)} %get-tuple-element.20), channel_id=1, source_target_pairs={{0,8},{8,16},{16,24},{24,32},{32,40},{40,48},{48,56},{1,9},{9,17},... | collective-permute-start | bytes 405512 | tf_op jit(solution)/shard_map/ppermute | solution.py:21
  54.4 79.6 %psum.21 = f32[16,16]{1,0:T(8,128)S(1)} all-reduce(f32[16,16]{1,0:T(8,128)S(1)} %fusion.141), channel_id=1, replica_groups=mesh['px'=4,'py'=8,'dom'=8] {'px','py','dom'}, use_global_device_ids=true, to_apply=%region_1.2 | all-reduce | flops 256 | bytes 2048 | tf_op jit(solution)/shard_map/psum | solution.py:191
  138.0 5.5 %all-to-all-start.3 = ((f32[8,2,8192]{2,1,0:T(2,128)}), f32[8,2,8192]{2,1,0:T(2,128)}, u32[]{:S(2)}, u32[]{:S(2)}) async-start(f32[8,2,8192]{2,1,0:T(2,128)} %copy.60), calls=%async_computation.3 | async-start | bytes 1048576 | tf_op jit(solution)/shard_map/all_to_all | solution.py:201
  147.2 3.1 %fusion.6 = f32[2,2,16,32,131]{4,3,2,1,0:T(8,128)} fusion(f32[2,2,22,38,128]{4,3,2,1,0:T(8,128)S(1)} %pad_maximum_fusion, f32[16,32,131]{2,1,0:T(8,128)S(1)} %fusion.101), kind=kLoop, calls=%fused_computation.20 | loop fusion | flops 1609728 | bytes 3053568 | tf_op jit(solution)/shard_map/mul | solution.py:48
  150.3 2.6 fusion.37
  152.9 8.6 %all-to-all-done.3 = f32[8,2,8192]{2,1,0:T(2,128)} async-done(((f32[8,2,8192]{2,1,0:T(2,128)}), f32[8,2,8192]{2,1,0:T(2,128)}, u32[]{:S(2)}, u32[]{:S(2)}) %all-to-all-start.3) | async-done | bytes 524320 | tf_op jit(solution)/shard_map/all_to_all | solution.py:201
  168.0 4.3 %fusion.84 = f32[2,2,16,32,128]{4,3,2,1,0:T(8,128)S(1)} fusion(f32[2,2,16,32,131]{4,3,2,1,0:T(8,128)} %fusion.6, f32[2,2,16,35,128]{4,3,2,1,0:T(8,128)S(1)} %copy-done.2, f32[2,2,19,32,128]{4,3,2,1,0:T(8,128)S(1)} %fusion.47, f32[1,2,16,32,128]{4,3,2,1,0:T(8,128)S(1)} %bitcast.82, f32[1,2,16,32,128]{4,3,2,1,0:T(8,128)S(1)} %bitcast.81, ...), kind=kLoop, calls=%fused_computation.153 | loop fusion | flops 6291456 | bytes 16252928 | tf_op jit(solution)/shard_map/add | solution.py:160
  175.1 3.2 %collective-permute-start.8 = (f32[2,2,3,32,128]{4,3,2,1,0:T(8,128)S(1)}, f32[2,2,3,32,128]{4,3,2,1,0:T(8,128)S(1)}, u32[]{:S(2)}, u32[]{:S(2)}) collective-permute-start(f32[2,2,3,32,128]{4,3,2,1,0:T(8,128)S(1)} %get-tuple-element.28), channel_id=1, source_target_pairs={{0,64},{64,128},{128,192},{1,65},{65,129},{129,193},{2,66},{66,130... | collective-permute-start | bytes 589832 | tf_op jit(solution)/shard_map/ppermute | solution.py:21
  178.3 2.5 fusion.1
  182.3 5.6 %collective-permute-start.10 = (f32[2,2,22,3,128]{4,3,2,1,0:T(4,128)S(1)}, f32[2,2,22,3,128]{4,3,2,1,0:T(4,128)S(1)}, u32[]{:S(2)}, u32[]{:S(2)}) collective-permute-start(f32[2,2,22,3,128]{4,3,2,1,0:T(4,128)S(1)} %get-tuple-element.18), channel_id=1, source_target_pairs={{0,8},{8,16},{16,24},{24,32},{32,40},{40,48},{48,56},{1,9},{9,17},... | collective-permute-start | bytes 405512 | tf_op jit(solution)/shard_map/ppermute | solution.py:21
  190.3 2.4 collective-permute-done.10
  199.4 3.5 %collective-permute-start.12 = (f32[2,2,3,32,128]{4,3,2,1,0:T(8,128)S(1)}, f32[2,2,3,32,128]{4,3,2,1,0:T(8,128)S(1)}, u32[]{:S(2)}, u32[]{:S(2)}) collective-permute-start(f32[2,2,3,32,128]{4,3,2,1,0:T(8,128)S(1)} %get-tuple-element.24), channel_id=1, source_target_pairs={{0,64},{64,128},{128,192},{1,65},{65,129},{129,193},{2,66},{66,130... | collective-permute-start | bytes 589832 | tf_op jit(solution)/shard_map/ppermute | solution.py:21
  202.9 2.5 fusion
  206.8 6.3 %collective-permute-start.14 = (f32[2,2,22,3,128]{4,3,2,1,0:T(4,128)S(1)}, f32[2,2,22,3,128]{4,3,2,1,0:T(4,128)S(1)}, u32[]{:S(2)}, u32[]{:S(2)}) collective-permute-start(f32[2,2,22,3,128]{4,3,2,1,0:T(4,128)S(1)} %get-tuple-element.16), channel_id=1, source_target_pairs={{0,8},{8,16},{16,24},{24,32},{32,40},{40,48},{48,56},{1,9},{9,17},... | collective-permute-start | bytes 405512 | tf_op jit(solution)/shard_map/ppermute | solution.py:21
  215.2 4.6 %collective-permute-done.14 = f32[2,2,22,3,128]{4,3,2,1,0:T(4,128)S(1)} collective-permute-done((f32[2,2,22,3,128]{4,3,2,1,0:T(4,128)S(1)}, f32[2,2,22,3,128]{4,3,2,1,0:T(4,128)S(1)}, u32[]{:S(2)}, u32[]{:S(2)}) %collective-permute-start.14) | collective-permute-done | bytes 135200 | tf_op jit(solution)/shard_map/ppermute | solution.py:21
  226.5 19.1 %psum.22 = f32[2]{0:T(128)S(1)} all-reduce(f32[2]{0:T(128)S(1)} %get-tuple-element.11), channel_id=1, replica_groups=mesh['px'=4,'py'=8,'dom'=8] {'py'}, use_global_device_ids=true, to_apply=%region_4.5 | all-reduce | flops 2 | bytes 16 | tf_op jit(solution)/shard_map/psum | solution.py:181
  245.7 9.2 %psum.23 = f32[2]{0:T(128)S(1)} all-reduce(f32[2]{0:T(128)S(1)} %psum.22), channel_id=1, replica_groups=mesh['px'=4,'py'=8,'dom'=8] {'px'}, use_global_device_ids=true, to_apply=%region_5.6 | all-reduce | flops 2 | bytes 16 | tf_op jit(solution)/shard_map/psum | solution.py:181
  255.5 19.2 %all_to_all.64 = f32[2,8,8192]{2,0,1:T(2,128)S(1)} all-to-all(f32[2,8,8192]{2,0,1:T(2,128)S(1)} %copy.55), channel_id=1, replica_groups=mesh['px'=4,'py'=8,'dom'=8] {'dom'}, dimensions={1} | all-to-all | bytes 1048576 | tf_op jit(solution)/shard_map/all_to_all | solution.py:185
  276.8 3.5 %all-to-all-start.2 = ((f32[8,2,8192]{2,1,0:T(2,128)}), f32[8,2,8192]{2,1,0:T(2,128)S(1)}, u32[]{:S(2)}, u32[]{:S(2)}) async-start(f32[8,2,8192]{2,1,0:T(2,128)} %copy.57), calls=%async_computation.2 | async-start | bytes 1048576 | tf_op jit(solution)/shard_map/all_to_all | solution.py:200
  281.1 15.1 %all-to-all-done.2 = f32[8,2,8192]{2,1,0:T(2,128)S(1)} async-done(((f32[8,2,8192]{2,1,0:T(2,128)}), f32[8,2,8192]{2,1,0:T(2,128)S(1)}, u32[]{:S(2)}, u32[]{:S(2)}) %all-to-all-start.2) | async-done | bytes 524320 | tf_op jit(solution)/shard_map/all_to_all | solution.py:200
  (140 shorter events, 62.8 us)
Async XLA Ops:
  0.6 13.2 %copy-start.8 = (f32[2,16,32,128]{3,2,1,0:T(8,128)S(1)}, f32[2,16,32,128]{3,2,1,0:T(8,128)}, u32[]{:S(2)}) copy-start(f32[2,16,32,128]{3,2,1,0:T(8,128)} %param.11) | copy-start | bytes 1572868
  2.5 37.5 %collective-permute-start.3 = (f32[2,2,3,32,128]{4,3,2,1,0:T(8,128)}, f32[2,2,3,32,128]{4,3,2,1,0:T(8,128)S(1)}, u32[]{:S(2)}, u32[]{:S(2)}) collective-permute-start(f32[2,2,3,32,128]{4,3,2,1,0:T(8,128)} %get-tuple-element.33), channel_id=1, source_target_pairs={{64,0},{128,64},{192,128},{65,1},{129,65},{193,129},{66,2},{130,66... | collective-permute-start | bytes 589832 | tf_op jit(solution)/shard_map/ppermute | solution.py:23
  7.6 32.4 %collective-permute-start.2 = (f32[2,2,3,32,128]{4,3,2,1,0:T(8,128)S(1)}, f32[2,2,3,32,128]{4,3,2,1,0:T(8,128)S(1)}, u32[]{:S(2)}, u32[]{:S(2)}) collective-permute-start(f32[2,2,3,32,128]{4,3,2,1,0:T(8,128)S(1)} %get-tuple-element.32), channel_id=1, source_target_pairs={{0,64},{64,128},{128,192},{1,65},{65,129},{129,193},{2,66},{66,130... | collective-permute-start | bytes 589832 | tf_op jit(solution)/shard_map/ppermute | solution.py:21
  9.5 22.0 %collective-permute-start = (f32[3,32,128]{2,1,0:T(8,128)S(1)}, f32[3,32,128]{2,1,0:T(8,128)S(1)}, u32[]{:S(2)}, u32[]{:S(2)}) collective-permute-start(f32[3,32,128]{2,1,0:T(8,128)S(1)} %get-tuple-element.39), channel_id=1, source_target_pairs={{0,64},{64,128},{128,192},{1,65},{65,129},{129,193},{2,66},{66,130... | collective-permute-start | bytes 147464 | tf_op jit(solution)/shard_map/ppermute | solution.py:21
  11.5 20.1 %collective-permute-start.1 = (f32[3,32,128]{2,1,0:T(8,128)S(1)}, f32[3,32,128]{2,1,0:T(8,128)S(1)}, u32[]{:S(2)}, u32[]{:S(2)}) collective-permute-start(f32[3,32,128]{2,1,0:T(8,128)S(1)} %get-tuple-element.38), channel_id=1, source_target_pairs={{64,0},{128,64},{192,128},{65,1},{129,65},{193,129},{66,2},{130,66... | collective-permute-start | bytes 147464 | tf_op jit(solution)/shard_map/ppermute | solution.py:23
  14.0 9.3 %copy-start.14 = (f32[2,3,1024]{2,0,1:T(2,128)S(1)}, f32[2,3,1024]{2,0,1:T(2,128)}, u32[]{:S(2)}) copy-start(f32[2,3,1024]{2,0,1:T(2,128)} %param.20) | copy-start | bytes 73732
  14.0 9.3 %copy-start.15 = (s32[6]{0:T(128)S(1)}, s32[6]{0:T(128)}, u32[]{:S(2)}) copy-start(s32[6]{0:T(128)} %param.21) | copy-start | bytes 76
  15.3 35.4 %all-to-all-start = ((f32[2,8,8192]{2,0,1:T(2,128)}), f32[2,8,8192]{2,0,1:T(2,128)S(1)}, u32[]{:S(2)}, u32[]{:S(2)}) async-start(f32[2,8,8192]{2,0,1:T(2,128)} %copy.54), calls=%async_computation | async-start | bytes 1048576 | tf_op jit(solution)/shard_map/all_to_all | solution.py:184
  31.6 7.6 %collective-permute-start.5 = (f32[22,3,128]{2,1,0:T(4,128)S(1)}, f32[22,3,128]{2,1,0:T(4,128)S(1)}, u32[]{:S(2)}, u32[]{:S(2)}) collective-permute-start(f32[22,3,128]{2,1,0:T(4,128)S(1)} %get-tuple-element.37), channel_id=1, source_target_pairs={{8,0},{16,8},{24,16},{32,24},{40,32},{48,40},{56,48},{9,1},{17,9},... | collective-permute-start | bytes 101384 | tf_op jit(solution)/shard_map/ppermute | solution.py:23
  32.9 6.6 %collective-permute-start.4 = (f32[22,3,128]{2,1,0:T(4,128)S(1)}, f32[22,3,128]{2,1,0:T(4,128)S(1)}, u32[]{:S(2)}, u32[]{:S(2)}) collective-permute-start(f32[22,3,128]{2,1,0:T(4,128)S(1)} %get-tuple-element.36), channel_id=1, source_target_pairs={{0,8},{8,16},{16,24},{24,32},{32,40},{40,48},{48,56},{1,9},{9,17},... | collective-permute-start | bytes 101384 | tf_op jit(solution)/shard_map/ppermute | solution.py:21
  40.0 10.6 %copy-start.4 = (f32[2,2,3,32,128]{4,3,2,1,0:T(8,128)}, f32[2,2,3,32,128]{4,3,2,1,0:T(8,128)S(1)}, u32[]{:S(2)}) copy-start(f32[2,2,3,32,128]{4,3,2,1,0:T(8,128)S(1)} %collective-permute-done.3) | copy-start | bytes 589828
  40.3 10.3 %copy-start.6 = (f32[2,2,3,32,128]{4,3,2,1,0:T(8,128)}, f32[2,2,3,32,128]{4,3,2,1,0:T(8,128)S(1)}, u32[]{:S(2)}) copy-start(f32[2,2,3,32,128]{4,3,2,1,0:T(8,128)S(1)} %collective-permute-done.2) | copy-start | bytes 589828
  41.2 104.7 %collective-permute-start.7 = (f32[2,2,22,3,128]{4,3,2,1,0:T(4,128)}, f32[2,2,22,3,128]{4,3,2,1,0:T(4,128)}, u32[]{:S(2)}, u32[]{:S(2)}) collective-permute-start(f32[2,2,22,3,128]{4,3,2,1,0:T(4,128)} %get-tuple-element.21), channel_id=1, source_target_pairs={{8,0},{16,8},{24,16},{32,24},{40,32},{48,40},{56,48},{9,1},{17,9},... | collective-permute-start | bytes 405512 | tf_op jit(solution)/shard_map/ppermute | solution.py:23
  42.5 103.4 %collective-permute-start.6 = (f32[2,2,22,3,128]{4,3,2,1,0:T(4,128)}, f32[2,2,22,3,128]{4,3,2,1,0:T(4,128)}, u32[]{:S(2)}, u32[]{:S(2)}) collective-permute-start(f32[2,2,22,3,128]{4,3,2,1,0:T(4,128)} %get-tuple-element.20), channel_id=1, source_target_pairs={{0,8},{8,16},{16,24},{24,32},{32,40},{40,48},{48,56},{1,9},{9,17},... | collective-permute-start | bytes 405512 | tf_op jit(solution)/shard_map/ppermute | solution.py:21
  138.0 23.5 %all-to-all-start.3 = ((f32[8,2,8192]{2,1,0:T(2,128)}), f32[8,2,8192]{2,1,0:T(2,128)}, u32[]{:S(2)}, u32[]{:S(2)}) async-start(f32[8,2,8192]{2,1,0:T(2,128)} %copy.60), calls=%async_computation.3 | async-start | bytes 1048576 | tf_op jit(solution)/shard_map/all_to_all | solution.py:201
  172.7 8.1 %collective-permute-start.9 = (f32[2,2,3,32,128]{4,3,2,1,0:T(8,128)S(1)}, f32[2,2,3,32,128]{4,3,2,1,0:T(8,128)S(1)}, u32[]{:S(2)}, u32[]{:S(2)}) collective-permute-start(f32[2,2,3,32,128]{4,3,2,1,0:T(8,128)S(1)} %get-tuple-element.29), channel_id=1, source_target_pairs={{64,0},{128,64},{192,128},{65,1},{129,65},{193,129},{66,2},{130,66... | collective-permute-start | bytes 589832 | tf_op jit(solution)/shard_map/ppermute | solution.py:23
  175.1 5.8 %collective-permute-start.8 = (f32[2,2,3,32,128]{4,3,2,1,0:T(8,128)S(1)}, f32[2,2,3,32,128]{4,3,2,1,0:T(8,128)S(1)}, u32[]{:S(2)}, u32[]{:S(2)}) collective-permute-start(f32[2,2,3,32,128]{4,3,2,1,0:T(8,128)S(1)} %get-tuple-element.28), channel_id=1, source_target_pairs={{0,64},{64,128},{128,192},{1,65},{65,129},{129,193},{2,66},{66,130... | collective-permute-start | bytes 589832 | tf_op jit(solution)/shard_map/ppermute | solution.py:21
  181.0 9.3 %collective-permute-start.11 = (f32[2,2,22,3,128]{4,3,2,1,0:T(4,128)S(1)}, f32[2,2,22,3,128]{4,3,2,1,0:T(4,128)S(1)}, u32[]{:S(2)}, u32[]{:S(2)}) collective-permute-start(f32[2,2,22,3,128]{4,3,2,1,0:T(4,128)S(1)} %get-tuple-element.19), channel_id=1, source_target_pairs={{8,0},{16,8},{24,16},{32,24},{40,32},{48,40},{56,48},{9,1},{17,9},... | collective-permute-start | bytes 405512 | tf_op jit(solution)/shard_map/ppermute | solution.py:23
  182.3 10.5 %collective-permute-start.10 = (f32[2,2,22,3,128]{4,3,2,1,0:T(4,128)S(1)}, f32[2,2,22,3,128]{4,3,2,1,0:T(4,128)S(1)}, u32[]{:S(2)}, u32[]{:S(2)}) collective-permute-start(f32[2,2,22,3,128]{4,3,2,1,0:T(4,128)S(1)} %get-tuple-element.18), channel_id=1, source_target_pairs={{0,8},{8,16},{16,24},{24,32},{32,40},{40,48},{48,56},{1,9},{9,17},... | collective-permute-start | bytes 405512 | tf_op jit(solution)/shard_map/ppermute | solution.py:21
  197.1 8.3 %collective-permute-start.13 = (f32[2,2,3,32,128]{4,3,2,1,0:T(8,128)S(1)}, f32[2,2,3,32,128]{4,3,2,1,0:T(8,128)S(1)}, u32[]{:S(2)}, u32[]{:S(2)}) collective-permute-start(f32[2,2,3,32,128]{4,3,2,1,0:T(8,128)S(1)} %get-tuple-element.25), channel_id=1, source_target_pairs={{64,0},{128,64},{192,128},{65,1},{129,65},{193,129},{66,2},{130,66... | collective-permute-start | bytes 589832 | tf_op jit(solution)/shard_map/ppermute | solution.py:23
  199.4 6.0 %collective-permute-start.12 = (f32[2,2,3,32,128]{4,3,2,1,0:T(8,128)S(1)}, f32[2,2,3,32,128]{4,3,2,1,0:T(8,128)S(1)}, u32[]{:S(2)}, u32[]{:S(2)}) collective-permute-start(f32[2,2,3,32,128]{4,3,2,1,0:T(8,128)S(1)} %get-tuple-element.24), channel_id=1, source_target_pairs={{0,64},{64,128},{128,192},{1,65},{65,129},{129,193},{2,66},{66,130... | collective-permute-start | bytes 589832 | tf_op jit(solution)/shard_map/ppermute | solution.py:21
  205.5 9.8 %collective-permute-start.15 = (f32[2,2,22,3,128]{4,3,2,1,0:T(4,128)S(1)}, f32[2,2,22,3,128]{4,3,2,1,0:T(4,128)S(1)}, u32[]{:S(2)}, u32[]{:S(2)}) collective-permute-start(f32[2,2,22,3,128]{4,3,2,1,0:T(4,128)S(1)} %get-tuple-element.17), channel_id=1, source_target_pairs={{8,0},{16,8},{24,16},{32,24},{40,32},{48,40},{56,48},{9,1},{17,9},... | collective-permute-start | bytes 405512 | tf_op jit(solution)/shard_map/ppermute | solution.py:23
  206.8 13.1 %collective-permute-start.14 = (f32[2,2,22,3,128]{4,3,2,1,0:T(4,128)S(1)}, f32[2,2,22,3,128]{4,3,2,1,0:T(4,128)S(1)}, u32[]{:S(2)}, u32[]{:S(2)}) collective-permute-start(f32[2,2,22,3,128]{4,3,2,1,0:T(4,128)S(1)} %get-tuple-element.16), channel_id=1, source_target_pairs={{0,8},{8,16},{16,24},{24,32},{32,40},{40,48},{48,56},{1,9},{9,17},... | collective-permute-start | bytes 405512 | tf_op jit(solution)/shard_map/ppermute | solution.py:21
  276.8 19.5 %all-to-all-start.2 = ((f32[8,2,8192]{2,1,0:T(2,128)}), f32[8,2,8192]{2,1,0:T(2,128)S(1)}, u32[]{:S(2)}, u32[]{:S(2)}) async-start(f32[8,2,8192]{2,1,0:T(2,128)} %copy.57), calls=%async_computation.2 | async-start | bytes 1048576 | tf_op jit(solution)/shard_map/all_to_all | solution.py:200
  (14 other events, 61.7 us)
